TPU v7x, 32 devices: a whole 2x2x4 slice. The times are simulated.
32 devices in a mesh: fsdp: 4 (over x, core), seq: 8 (over z, y).
Axes of the slice: x: 2, y: 2, z: 4, core: 2. Of those that a mesh axis runs over, the one named last changes fastest.
Arguments:
- tokens: bfloat16 [4, 56, 28, 512], P('fsdp', 'seq'), may hold values from -6 to 6
- cotangent: bfloat16 [4, 56, 28, 512], P('fsdp', 'seq'), may hold values from -6 to 6
- region_ids: int32 [56, 28], replicated, may hold values from 0 to 3
- relative_index: int32 [49, 49], replicated, may hold values from 0 to 168, as said below
- first_gain: bfloat16 [512], P('fsdp'), may hold values from 0.5 to 1.5
- first_offset: bfloat16 [512], P('fsdp'), may hold values from -3 to 3
- qkv_weight: bfloat16 [512, 1536], P('fsdp'), may hold values from -0.25 to 0.25
- proj_weight: bfloat16 [512, 512], P('fsdp'), may hold values from -0.75 to 0.75
- bias_table: bfloat16 [16, 169], P('fsdp'), may hold values from -4 to 4
- second_gain: bfloat16 [512], P('fsdp'), may hold values from 0.5 to 1.5
- second_offset: bfloat16 [512], P('fsdp'), may hold values from -3 to 3
- expand_weight: bfloat16 [512, 2048], P('fsdp'), may hold values from -0.25 to 0.25
- reduce_weight: bfloat16 [2048, 512], P('fsdp'), may hold values from -0.125 to 0.125
Outputs:
- output: bfloat16 [4, 56, 28, 512], P('fsdp', 'seq')
- tokens_grad: float32 [4, 56, 28, 512], P('fsdp', 'seq')
- first_gain_grad: float32 [512], P('fsdp')
- first_offset_grad: float32 [512], P('fsdp')
- qkv_weight_grad: float32 [512, 1536], P('fsdp')
- proj_weight_grad: float32 [512, 512], P('fsdp')
- bias_table_grad: float32 [16, 169], P('fsdp')
- second_gain_grad: float32 [512], P('fsdp')
- second_offset_grad: float32 [512], P('fsdp')
- expand_weight_grad: float32 [512, 2048], P('fsdp')
- reduce_weight_grad: float32 [2048, 512], P('fsdp')
Inputs may be any that keep to these rules, and one draw needn't show every extreme that they name: relative_index[i, j] depends only on the row and column offsets between positions i and j of a 7 x 7 window, and distinct offsets give distinct entries.
All inputs are finite; a program needn't handle non-finite values.
Results may differ from a plain program's by a relative error of at most 0.018.
Values may be sent and summed in bfloat16 or wider, within the bound.
A program may use at most 128 MiB of HBM per device.

v0:
```python
import jax
import jax.numpy as jnp
from jax import lax
from jax.sharding import PartitionSpec as P

WS = 7
SHIFT = 3
EPSILON = 1e-05
MASKED = -100.0
SQRT_HALF = 0.7071067811865476
INV_ROOT_TAU = 0.3989422804014327


def layer_norm(values, norm_gain, norm_offset):
    average = jnp.mean(values, axis=-1, keepdims=True)
    centred = values - average
    variance = jnp.mean(centred * centred, axis=-1, keepdims=True)
    inverse = lax.rsqrt(variance + EPSILON)
    normed = centred * inverse
    return (normed * norm_gain + norm_offset, normed, inverse)


def norm_back(upstream, normed, inverse, norm_gain):
    scaled = upstream * norm_gain
    mean_grad = jnp.mean(scaled, axis=-1, keepdims=True)
    second = jnp.mean(scaled * normed, axis=-1, keepdims=True)
    grad_in = inverse * (scaled - mean_grad - normed * second)
    lead_axes = tuple(range(upstream.ndim - 1))
    return (grad_in, jnp.sum(upstream * normed, axis=lead_axes), jnp.sum(upstream, axis=lead_axes))


def gelu_parts(hidden):
    normal_cdf = 0.5 * (1.0 + jax.scipy.special.erf(hidden * SQRT_HALF))
    density = jnp.exp(-0.5 * hidden * hidden) * INV_ROOT_TAU
    return (hidden * normal_cdf, normal_cdf + hidden * density)


def to_windows(field_in, num_heads):
    lead_dims = field_in.shape[:-3]
    num_rows, num_cols, features = field_in.shape[-3:]
    lead_count = len(lead_dims)
    pieces = field_in.reshape(
        lead_dims + (num_rows // WS, WS, num_cols // WS, WS, num_heads, features // num_heads)
    )
    axis_order = tuple(range(lead_count)) + (
        lead_count,
        lead_count + 2,
        lead_count + 4,
        lead_count + 1,
        lead_count + 3,
        lead_count + 5,
    )
    return pieces.transpose(axis_order).reshape(
        lead_dims + (num_rows // WS, num_cols // WS, num_heads, WS * WS, features // num_heads)
    )


def from_windows(window_tiles):
    lead_dims = window_tiles.shape[:-5]
    win_rows, win_cols, num_heads, positions, head_dim = window_tiles.shape[-5:]
    lead_count = len(lead_dims)
    pieces = window_tiles.reshape(lead_dims + (win_rows, win_cols, num_heads, WS, WS, head_dim))
    axis_order = tuple(range(lead_count)) + (
        lead_count,
        lead_count + 3,
        lead_count + 1,
        lead_count + 4,
        lead_count + 2,
        lead_count + 5,
    )
    return pieces.transpose(axis_order).reshape(
        lead_dims + (win_rows * WS, win_cols * WS, num_heads * head_dim)
    )


def make_mask(regions):
    num_rows, num_cols = regions.shape
    region_tiles = (
        regions.reshape(num_rows // WS, WS, num_cols // WS, WS)
        .transpose(0, 2, 1, 3)
        .reshape(num_rows // WS, num_cols // WS, WS * WS)
    )
    same_region = region_tiles[..., :, None] == region_tiles[..., None, :]
    return jnp.where(same_region, 0.0, MASKED).astype(jnp.float32)


def one_hot_index(relative_index, entries):
    return (relative_index[..., None] == jnp.arange(entries, dtype=jnp.int32)).astype(jnp.float32)


def table_bias(table_rows, relative_index):
    onehot = one_hot_index(relative_index, table_rows.shape[-1])
    return jnp.einsum("ijr,hr->hij", onehot, table_rows, precision=lax.Precision.HIGHEST)


def table_grad(bias_grad, relative_index, entries):
    onehot = one_hot_index(relative_index, entries)
    return jnp.einsum("hij,ijr->hr", bias_grad, onehot, precision=lax.Precision.HIGHEST)


def attend_forward(qkv_field, rel_bias, mask_add, num_heads):
    rolled = jnp.roll(qkv_field, -SHIFT, axis=-2)
    window_tiles = to_windows(rolled, num_heads)
    queries, key_tiles, value_tiles = (window_tiles[:, 0], window_tiles[:, 1], window_tiles[:, 2])
    scores = (
        jnp.einsum("bxyhid,bxyhjd->bxyhij", queries, key_tiles, preferred_element_type=jnp.float32)
        + rel_bias
        + mask_add[:, :, None]
    )
    exp_scores = jnp.exp(scores)
    row_total = jnp.sum(exp_scores, axis=-1, keepdims=True)
    attn_probs = (exp_scores / row_total).astype(jnp.bfloat16)
    attn_tiles = jnp.einsum(
        "bxyhij,bxyhjd->bxyhid", attn_probs, value_tiles, preferred_element_type=jnp.float32
    ).astype(jnp.bfloat16)
    field_out = jnp.roll(from_windows(attn_tiles), SHIFT, axis=-2)
    return (field_out, (queries, key_tiles, value_tiles, jnp.log(row_total)))


def attend_backward(grad_field, kept_state, rel_bias, mask_add, num_heads):
    queries, key_tiles, value_tiles, log_total = kept_state
    grad_tiles = to_windows(jnp.roll(grad_field, -SHIFT, axis=-2), num_heads)
    scores = (
        jnp.einsum("bxyhid,bxyhjd->bxyhij", queries, key_tiles, preferred_element_type=jnp.float32)
        + rel_bias
        + mask_add[:, :, None]
    )
    probs_back = jnp.exp(scores - log_total)
    value_grad = jnp.einsum(
        "bxyhij,bxyhid->bxyhjd",
        probs_back.astype(jnp.bfloat16),
        grad_tiles,
        preferred_element_type=jnp.float32,
    )
    prob_grad = jnp.einsum(
        "bxyhid,bxyhjd->bxyhij", grad_tiles, value_tiles, preferred_element_type=jnp.float32
    )
    score_grad = probs_back * (prob_grad - jnp.sum(probs_back * prob_grad, axis=-1, keepdims=True))
    score_low = score_grad.astype(jnp.bfloat16)
    query_scale = queries.shape[-1] ** (-0.5)
    query_grad = (
        jnp.einsum(
            "bxyhij,bxyhjd->bxyhid", score_low, key_tiles, preferred_element_type=jnp.float32
        )
        * query_scale
    )
    key_grad = jnp.einsum(
        "bxyhij,bxyhid->bxyhjd", score_low, queries, preferred_element_type=jnp.float32
    )
    stacked = jnp.stack([query_grad, key_grad, value_grad], axis=1).astype(jnp.bfloat16)
    field_grad = jnp.roll(from_windows(stacked), SHIFT, axis=-2)
    return (field_grad, jnp.sum(score_grad, axis=(0, 1, 2)))


def shards(
    tokens,
    cotangent,
    region_ids,
    relative_index,
    first_gain,
    first_offset,
    qkv_weight,
    proj_weight,
    bias_table,
    second_gain,
    second_offset,
    expand_weight,
    reduce_weight,
):
    gathered = (
        lax.all_gather(first_gain, "fsdp", axis=0, tiled=True),
        lax.all_gather(first_offset, "fsdp", axis=0, tiled=True),
        lax.all_gather(qkv_weight, "fsdp", axis=0, tiled=True),
        lax.all_gather(proj_weight, "fsdp", axis=0, tiled=True),
        lax.all_gather(bias_table, "fsdp", axis=0, tiled=True),
        lax.all_gather(second_gain, "fsdp", axis=0, tiled=True),
        lax.all_gather(second_offset, "fsdp", axis=0, tiled=True),
        lax.all_gather(expand_weight, "fsdp", axis=0, tiled=True),
        lax.all_gather(reduce_weight, "fsdp", axis=0, tiled=True),
    )
    gain_one = gathered[0].astype(jnp.float32)
    offset_one = gathered[1].astype(jnp.float32)
    qkv_full = gathered[2]
    proj_full = gathered[3]
    table_full = gathered[4].astype(jnp.float32)
    gain_two = gathered[5].astype(jnp.float32)
    offset_two = gathered[6].astype(jnp.float32)
    expand_full = gathered[7]
    reduce_full = gathered[8]
    num_images, num_rows, num_cols, width = tokens.shape
    num_heads, entries = table_full.shape
    query_scale = (width // num_heads) ** (-0.5)
    factors = jnp.array([query_scale, 1.0, 1.0], dtype=jnp.float32).reshape(1, 3, 1, 1, 1)
    qkv_cols = qkv_full.reshape(width, 3, width)
    inputs = tokens.astype(jnp.float32)
    normed_one, hat_one, inv_one = layer_norm(inputs, gain_one, offset_one)
    first_low = normed_one.astype(jnp.bfloat16)
    per_device = num_heads // lax.axis_size("seq")
    head_start = lax.axis_index("seq") * per_device
    qkv_local = (
        jnp.einsum("brwc,ctd->btrwd", first_low, qkv_cols, preferred_element_type=jnp.float32)
        * factors
    ).astype(jnp.bfloat16)
    qkv_heads = lax.all_to_all(qkv_local, "seq", split_axis=4, concat_axis=2, tiled=True)
    qkv_heads = jnp.roll(qkv_heads, -SHIFT, axis=2)
    rel_bias = table_bias(
        lax.dynamic_slice_in_dim(table_full, head_start, per_device, 0), relative_index
    )
    mask_add = make_mask(region_ids)
    attn_heads, kept_state = attend_forward(qkv_heads, rel_bias, mask_add, per_device)
    attn_heads = jnp.roll(attn_heads, SHIFT, axis=1)
    attended = lax.all_to_all(attn_heads, "seq", split_axis=1, concat_axis=3, tiled=True)
    middle = inputs + jnp.einsum(
        "brwc,cd->brwd", attended, proj_full, preferred_element_type=jnp.float32
    )
    normed_two, hat_two, inv_two = layer_norm(middle, gain_two, offset_two)
    second_low = normed_two.astype(jnp.bfloat16)
    hidden = jnp.einsum(
        "brwc,cf->brwf", second_low, expand_full, preferred_element_type=jnp.float32
    )
    activated, slope = gelu_parts(hidden)
    act_low = activated.astype(jnp.bfloat16)
    output = (
        middle
        + jnp.einsum("brwf,fc->brwc", act_low, reduce_full, preferred_element_type=jnp.float32)
    ).astype(jnp.bfloat16)
    reduce_grad = jnp.einsum(
        "brwf,brwc->fc", act_low, cotangent, preferred_element_type=jnp.float32
    )
    hidden_grad = (
        jnp.einsum("brwc,fc->brwf", cotangent, reduce_full, preferred_element_type=jnp.float32)
        * slope
    ).astype(jnp.bfloat16)
    expand_grad = jnp.einsum(
        "brwc,brwf->cf", second_low, hidden_grad, preferred_element_type=jnp.float32
    )
    upstream_two = jnp.einsum(
        "brwf,cf->brwc", hidden_grad, expand_full, preferred_element_type=jnp.float32
    )
    back_two, gain_two_grad, offset_two_grad = norm_back(upstream_two, hat_two, inv_two, gain_two)
    middle_grad = cotangent.astype(jnp.float32) + back_two
    middle_low = middle_grad.astype(jnp.bfloat16)
    proj_grad = jnp.einsum(
        "brwc,brwd->cd", attended, middle_low, preferred_element_type=jnp.float32
    )
    attended_grad = jnp.einsum(
        "brwd,cd->brwc", middle_low, proj_full, preferred_element_type=jnp.float32
    ).astype(jnp.bfloat16)
    grad_heads = lax.all_to_all(attended_grad, "seq", split_axis=3, concat_axis=1, tiled=True)
    grad_heads = jnp.roll(grad_heads, -SHIFT, axis=1)
    qkv_grad_heads, bias_grad = attend_backward(
        grad_heads, kept_state, rel_bias, mask_add, per_device
    )
    qkv_grad_heads = jnp.roll(qkv_grad_heads, SHIFT, axis=2)
    qkv_grad = lax.all_to_all(qkv_grad_heads, "seq", split_axis=2, concat_axis=4, tiled=True)
    table_part = table_grad(bias_grad, relative_index, entries)
    table_grads = lax.dynamic_update_slice(
        jnp.zeros((num_heads, entries), jnp.float32), table_part, (head_start, 0)
    )
    qkv_grad_w = jnp.einsum(
        "brwc,btrwd->ctd", first_low, qkv_grad, preferred_element_type=jnp.float32
    ).reshape(width, 3 * width)
    upstream_one = jnp.einsum(
        "btrwd,ctd->brwc", qkv_grad, qkv_cols, preferred_element_type=jnp.float32
    )
    back_one, gain_one_grad, offset_one_grad = norm_back(upstream_one, hat_one, inv_one, gain_one)
    tokens_grad = middle_grad + back_one
    shares = (
        lax.psum_scatter(
            gain_one_grad.astype(jnp.bfloat16), "fsdp", scatter_dimension=0, tiled=True
        ).astype(jnp.float32),
        lax.psum_scatter(
            offset_one_grad.astype(jnp.bfloat16), "fsdp", scatter_dimension=0, tiled=True
        ).astype(jnp.float32),
        lax.psum_scatter(
            qkv_grad_w.astype(jnp.bfloat16), "fsdp", scatter_dimension=0, tiled=True
        ).astype(jnp.float32),
        lax.psum_scatter(
            proj_grad.astype(jnp.bfloat16), "fsdp", scatter_dimension=0, tiled=True
        ).astype(jnp.float32),
        lax.psum_scatter(
            table_grads.astype(jnp.bfloat16), "fsdp", scatter_dimension=0, tiled=True
        ).astype(jnp.float32),
        lax.psum_scatter(
            gain_two_grad.astype(jnp.bfloat16), "fsdp", scatter_dimension=0, tiled=True
        ).astype(jnp.float32),
        lax.psum_scatter(
            offset_two_grad.astype(jnp.bfloat16), "fsdp", scatter_dimension=0, tiled=True
        ).astype(jnp.float32),
        lax.psum_scatter(
            expand_grad.astype(jnp.bfloat16), "fsdp", scatter_dimension=0, tiled=True
        ).astype(jnp.float32),
        lax.psum_scatter(
            reduce_grad.astype(jnp.bfloat16), "fsdp", scatter_dimension=0, tiled=True
        ).astype(jnp.float32),
    )
    totals = (
        lax.psum(shares[0].astype(jnp.bfloat16), "seq").astype(jnp.float32),
        lax.psum(shares[1].astype(jnp.bfloat16), "seq").astype(jnp.float32),
        lax.psum(shares[2].astype(jnp.bfloat16), "seq").astype(jnp.float32),
        lax.psum(shares[3].astype(jnp.bfloat16), "seq").astype(jnp.float32),
        lax.psum(shares[4].astype(jnp.bfloat16), "seq").astype(jnp.float32),
        lax.psum(shares[5].astype(jnp.bfloat16), "seq").astype(jnp.float32),
        lax.psum(shares[6].astype(jnp.bfloat16), "seq").astype(jnp.float32),
        lax.psum(shares[7].astype(jnp.bfloat16), "seq").astype(jnp.float32),
        lax.psum(shares[8].astype(jnp.bfloat16), "seq").astype(jnp.float32),
    )
    qkv_total = totals[2]
    proj_total = totals[3]
    expand_total = totals[7]
    reduce_total = totals[8]
    return (
        output,
        tokens_grad,
        totals[0],
        totals[1],
        qkv_total,
        proj_total,
        totals[4],
        totals[5],
        totals[6],
        expand_total,
        reduce_total,
    )


def solution(mesh):
    placed = (
        P("fsdp", "seq", None, None),
        P("fsdp", "seq", None, None),
        P(),
        P(),
        P("fsdp"),
        P("fsdp"),
        P("fsdp", None),
        P("fsdp", None),
        P("fsdp", None),
        P("fsdp"),
        P("fsdp"),
        P("fsdp", None),
        P("fsdp", None),
    )
    return jax.shard_map(
        shards,
        mesh=mesh,
        in_specs=placed,
        out_specs=(
            P("fsdp", "seq", None, None),
            P("fsdp", "seq", None, None),
            P("fsdp"),
            P("fsdp"),
            P("fsdp", None),
            P("fsdp", None),
            P("fsdp", None),
            P("fsdp"),
            P("fsdp"),
            P("fsdp", None),
            P("fsdp", None),
        ),
        check_vma=False,
    )
```

profile of v0, /device:TPU:0, one launch (start us, length us, event | category | flops | bytes accessed | tf_op | source)
XLA Modules:
  0.0 359.1 jit_solution(13753991665746310214)
XLA Ops:
  10.0 6.2 %all-gather = bf16[4,1,128]{2,1,0:T(2,128)(2,1)S(1)} all-gather(bf16[1,1,128]{2,1,0:T(2,128)(2,1)} %bitcast.275), channel_id=1, replica_groups=mesh['fsdp'=4,'seq'=8] {'fsdp'}, dimensions={0}, use_global_device_ids=true | all-gather | bytes 1280 | tf_op jit(solution)/shard_map/all_gather | solution.py:171
  16.2 5.4 %all-gather.1 = bf16[4,1,128]{2,1,0:T(2,128)(2,1)S(1)} all-gather(bf16[1,1,128]{2,1,0:T(2,128)(2,1)} %bitcast.276), channel_id=1, replica_groups=mesh['fsdp'=4,'seq'=8] {'fsdp'}, dimensions={0}, use_global_device_ids=true | all-gather | bytes 1280 | tf_op jit(solution)/shard_map/all_gather | solution.py:172
  22.0 10.7 %all-gather.9.cloned.1.call-done = bf16[512,1536]{0,1:T(8,128)(2,1)} async-done(((bf16[128,1536]{0,1:T(8,128)(2,1)}), bf16[512,1536]{0,1:T(8,128)(2,1)}) %all-gather.9.cloned.1.call-update) | async-done | bytes 1572880 | tf_op jit(solution)/shard_map/all_gather | solution.py:173
  32.7 2.9 fusion.22
  35.6 3.7 %copy.100 = bf16[1,3,7,28,512]{3,2,1,0,4:T(8,128)(2,1)S(1)} copy(bf16[1,3,7,28,512]{4,3,1,2,0:T(8,128)(2,1)} %fusion.22) | data formatting | bytes 1204224 | tf_op jit(solution)/shard_map/convert_element_type | solution.py:203
  39.4 4.6 %reshape.406 = bf16[8,2,18816]{2,1,0:T(2,128)(2,1)} reshape(bf16[512,1,3,7,28]{4,3,2,1,0:T(8,128)(2,1)S(1)} %bitcast.239) | data formatting | bytes 1204224
  44.0 5.6 %all-to-all-start = ((bf16[8,2,18816]{2,1,0:T(2,128)(2,1)}), bf16[8,2,18816]{2,1,0:T(2,128)(2,1)}, u32[]{:S(2)}, u32[]{:S(2)}) async-start(bf16[8,2,18816]{2,1,0:T(2,128)(2,1)} %reshape.406), calls=%async_computation | async-start | bytes 1204224 | tf_op jit(solution)/shard_map/all_to_all | solution.py:204
  50.4 5.4 %all-gather.2 = bf16[4,4,169]{2,1,0:T(4,128)(2,1)S(1)} all-gather(bf16[1,4,169]{2,1,0:T(4,128)(2,1)S(1)} %bitcast.272), channel_id=1, replica_groups=mesh['fsdp'=4,'seq'=8] {'fsdp'}, dimensions={0}, use_global_device_ids=true | all-gather | bytes 6760 | tf_op jit(solution)/shard_map/all_gather | solution.py:175
  58.4 7.9 %all-to-all-done = bf16[8,2,18816]{2,1,0:T(2,128)(2,1)} async-done(((bf16[8,2,18816]{2,1,0:T(2,128)(2,1)}), bf16[8,2,18816]{2,1,0:T(2,128)(2,1)}, u32[]{:S(2)}, u32[]{:S(2)}) %all-to-all-start) | async-done | bytes 602144 | tf_op jit(solution)/shard_map/all_to_all | solution.py:204
  66.3 5.0 %reshape.407 = bf16[512,1,3,7,28]{4,3,2,1,0:T(8,128)(2,1)S(1)} reshape(bf16[8,2,18816]{2,1,0:T(2,128)(2,1)} %all-to-all-done) | data formatting | bytes 1204224
  71.3 4.5 %copy.101 = bf16[1,3,7,28,8,64]{5,2,4,3,1,0:T(8,128)(2,1)} copy(bf16[1,3,7,28,8,64]{3,2,1,5,4,0:T(8,128)(2,1)S(1)} %bitcast.238) | data formatting | bytes 1204224 | tf_op jit(solution)/shard_map/all_to_all | solution.py:204
  75.8 2.4 all_to_all.51
  80.4 4.3 %reshape.357 = bf16[1,3,8,7,4,7,2,32]{7,6,3,2,5,4,1,0:T(2,128)(2,1)S(1)} reshape(bf16[1,3,56,28,64]{4,2,3,1,0:T(8,128)(2,1)} %fusion.27) | data formatting | bytes 1204224 | tf_op jit(solution)/shard_map/reshape | solution.py:42
  98.7 3.7 %all-to-all-start.1 = ((bf16[8,2,6272]{2,1,0:T(2,128)(2,1)}), bf16[8,2,6272]{2,1,0:T(2,128)(2,1)S(1)}, u32[]{:S(2)}, u32[]{:S(2)}) async-start(bf16[8,2,6272]{2,1,0:T(2,128)(2,1)} %reshape.408), calls=%async_computation.1 | async-start | bytes 401408 | tf_op jit(solution)/shard_map/all_to_all | solution.py:212
  102.4 5.1 %all-gather.3 = bf16[4,1,128]{2,1,0:T(2,128)(2,1)S(1)} all-gather(bf16[1,1,128]{2,1,0:T(2,128)(2,1)S(1)} %bitcast.277), channel_id=1, replica_groups=mesh['fsdp'=4,'seq'=8] {'fsdp'}, dimensions={0}, use_global_device_ids=true | all-gather | bytes 1280 | tf_op jit(solution)/shard_map/all_gather | solution.py:176
  107.4 5.0 %all-gather.4 = bf16[4,1,128]{2,1,0:T(2,128)(2,1)S(1)} all-gather(bf16[1,1,128]{2,1,0:T(2,128)(2,1)S(1)} %bitcast.278), channel_id=1, replica_groups=mesh['fsdp'=4,'seq'=8] {'fsdp'}, dimensions={0}, use_global_device_ids=true | all-gather | bytes 1280 | tf_op jit(solution)/shard_map/all_gather | solution.py:177
  112.5 7.9 %all_gather.31 = bf16[512,512]{1,0:T(8,128)(2,1)S(1)} all-gather(bf16[128,512]{1,0:T(8,128)(2,1)S(1)} %copy-done.22), channel_id=1, replica_groups=mesh['fsdp'=4,'seq'=8] {'fsdp'}, dimensions={0}, use_global_device_ids=true | all-gather | bytes 655360 | tf_op jit(solution)/shard_map/all_gather | solution.py:174
  121.9 4.0 %multiply_convert_fusion = (bf16[7,28,2048]{2,1,0:T(8,128)(2,1)}, f32[7,28,2048]{2,1,0:T(8,128)}) fusion(bf16[512,2048]{1,0:T(8,128)(2,1)} %all-gather.11.cloned.1.call-done, f32[1,7,28,512]{3,2,1,0:T(8,128)S(1)} %get-tuple-element.85, f32[512]{0:T(512)S(1)} %bitcast.270, f32[512]{0:T(512)S(1)} %bitcast.260, f32[7,28]{1,0:T(8,128)S(1)} %add_rsqrt_fusion, ...), kind=kOutput, calls=%fused_computation.25 | convolution fusion | flops 413550592 | bytes 4912672 | tf_op jit(solution)/shard_map/brwc,cf->brwf/dot_general | solution.py:218
  125.9 3.3 fusion.3
  132.7 3.4 bitcast_convert_fusion.1
  137.0 3.3 bitcast_convert_fusion
  145.0 5.9 %all-to-all-start.2 = ((bf16[8,2,6272]{2,1,0:T(2,128)(2,1)}), bf16[8,2,6272]{2,1,0:T(2,128)(2,1)S(1)}, u32[]{:S(2)}, u32[]{:S(2)}) async-start(bf16[8,2,6272]{2,1,0:T(2,128)(2,1)} %reshape.410), calls=%async_computation.2 | async-start | bytes 401408 | tf_op jit(solution)/shard_map/all_to_all | solution.py:249
  152.6 6.9 %all-to-all-done.2 = bf16[8,2,6272]{2,1,0:T(2,128)(2,1)S(1)} async-done(((bf16[8,2,6272]{2,1,0:T(2,128)(2,1)}), bf16[8,2,6272]{2,1,0:T(2,128)(2,1)S(1)}, u32[]{:S(2)}, u32[]{:S(2)}) %all-to-all-start.2) | async-done | bytes 200736 | tf_op jit(solution)/shard_map/all_to_all | solution.py:249
  168.6 2.4 copy.126
  180.3 2.3 reshape.371
  185.5 19.8 %all_to_all.66 = bf16[8,2,18816]{2,1,0:T(2,128)(2,1)S(1)} all-to-all(bf16[8,2,18816]{2,1,0:T(2,128)(2,1)S(1)} %reshape.412), channel_id=1, replica_groups=mesh['fsdp'=4,'seq'=8] {'seq'}, dimensions={0} | all-to-all | bytes 1204224 | tf_op jit(solution)/shard_map/all_to_all | solution.py:255
  213.1 9.0 %reduce-scatter.11.cloned.1.call-done = bf16[512,512]{1,0:T(8,128)(2,1)} async-done(((bf16[2048,512]{1,0:T(8,128)(2,1)}), bf16[512,512]{1,0:T(8,128)(2,1)}) %reduce-scatter.11.cloned.1.call-update) | async-done | bytes 524304 | tf_op jit(solution)/shard_map/reduce_scatter | solution.py:293
  222.1 30.6 %reduce-scatter.5.cloned.1.call-done = bf16[128,1536]{1,0:T(8,128)(2,1)} async-done(((bf16[512,1536]{1,0:T(8,128)(2,1)}), bf16[128,1536]{1,0:T(8,128)(2,1)}) %reduce-scatter.5.cloned.1.call-update) | async-done | bytes 393232 | tf_op jit(solution)/shard_map/reduce_scatter | solution.py:275
  252.7 2.9 fusion.32
  259.1 10.5 %all-reduce.7 = (bf16[512]{0:T(512)(128)(2,1)S(1)}, bf16[512]{0:T(512)(128)(2,1)S(1)}, bf16[16,169]{1,0:T(8,128)(2,1)S(1)}, bf16[512]{0:T(512)(128)(2,1)S(1)}, bf16[512]{0:T(512)(128)(2,1)S(1)}) all-reduce(bf16[512]{0:T(512)(128)(2,1)S(1)} %get-tuple-element.57, ...), channel_id=2, replica_groups=mesh['fsdp'=4,'seq'=8] {'fsdp'}, use_global_device_ids=true, to_apply=%region_11.12.clone | all-reduce | flops 4752 | bytes 19008
  270.0 21.9 %all-reduce.5 = (bf16[128]{0:T(256)(128)(2,1)S(1)}, bf16[128]{0:T(256)(128)(2,1)S(1)}, bf16[4,169]{1,0:T(4,128)(2,1)S(1)}, bf16[128]{0:T(256)(128)(2,1)S(1)}, bf16[128]{0:T(256)(128)(2,1)S(1)}) all-reduce(bf16[128]{0:T(256)(128)(2,1)S(1)} %dynamic-slice.1, ...), channel_id=1, replica_groups=mesh['fsdp'=4,'seq'=8] {'seq'}, use_global_device_ids=true, to_apply=%region_12.13 | all-reduce | flops 1188 | bytes 4752 | tf_op jit(solution)/shard_map/psum | solution.py:298
  295.9 50.3 %all-reduce.10.cloned.1.call-done = (bf16[128,1536]{1,0:T(8,128)(2,1)}, bf16[128,512]{1,0:T(8,128)(2,1)}, bf16[128,2048]{1,0:T(8,128)(2,1)}, bf16[512,512]{1,0:T(8,128)(2,1)}) async-done(((bf16[128,1536]{1,0:T(8,128)(2,1)}, bf16[128,512]{1,0:T(8,128)(2,1)}, bf16[128,2048]{1,0:T(8,128)(2,1)}, bf16[512,512]{1,0:T(8,128)(2,1)}), (bf16[128,1536]{1,0:T(8,128)(2,1)}, bf16[128,512]{1,0:T(8,128)(2,1)}, ...) | async-done | bytes 1572880 | tf_op jit(solution)/shard_map/psum | solution.py:300
  (202 shorter events, 75.8 us)
Async XLA Ops:
  7.2 25.5 %copy-start.34 = (f32[3]{0:T(128)S(1)}, f32[3]{0:T(128)}, u32[]{:S(2)}) copy-start(f32[3]{0:T(128)} %constant.41.clone) | copy-start | bytes 40
  7.2 14.5 %copy-start.7 = (bf16[1,7,28,512]{3,2,1,0:T(8,128)(2,1)S(1)}, bf16[1,7,28,512]{3,2,1,0:T(8,128)(2,1)}, u32[]{:S(2)}) copy-start(bf16[1,7,28,512]{3,2,1,0:T(8,128)(2,1)} %param.14) | copy-start | bytes 602116
  7.2 25.5 %all-gather.9.cloned.1.call-start = ((), (), s32[]{:S(2)}) async-start(), calls=%async_computation.8 | async-start | bytes 1966080 | tf_op jit(solution)/shard_map/all_gather | solution.py:173
  9.2 112.7 %all-gather.11.cloned.1.call-start = ((), (), s32[]{:S(2)}) async-start(), calls=%async_computation.9 | async-start | bytes 2621440 | tf_op jit(solution)/shard_map/all_gather | solution.py:178
  21.6 11.1 %copy-start.26 = (f32[4,1,128]{2,1,0:T(1,128)}, f32[4,1,128]{2,1,0:T(1,128)S(1)}, u32[]{:S(2)}) copy-start(f32[4,1,128]{2,1,0:T(1,128)S(1)} %convert_element_type.190) | copy-start | bytes 6148
  39.4 11.0 %copy-start.25 = (bf16[4,169]{1,0:T(4,128)(2,1)S(1)}, bf16[4,169]{1,0:T(4,128)(2,1)}, u32[]{:S(2)}) copy-start(bf16[4,169]{1,0:T(4,128)(2,1)} %param.22) | copy-start | bytes 4060
  39.4 16.4 %copy-start.31 = (s32[49,49]{1,0:T(8,128)S(1)}, s32[49,49]{1,0:T(8,128)}, u32[]{:S(2)}) copy-start(s32[49,49]{1,0:T(8,128)} %param.17) | copy-start | bytes 28816
  44.0 12.7 %copy-start.23 = (s32[56,28]{0,1:T(8,128)S(1)}, s32[56,28]{0,1:T(8,128)}, u32[]{:S(2)}) copy-start(s32[56,28]{0,1:T(8,128)} %param.16) | copy-start | bytes 18820
  44.0 22.3 %all-to-all-start = ((bf16[8,2,18816]{2,1,0:T(2,128)(2,1)}), bf16[8,2,18816]{2,1,0:T(2,128)(2,1)}, u32[]{:S(2)}, u32[]{:S(2)}) async-start(bf16[8,2,18816]{2,1,0:T(2,128)(2,1)} %reshape.406), calls=%async_computation | async-start | bytes 1204224 | tf_op jit(solution)/shard_map/all_to_all | solution.py:204
  49.6 76.3 %all-gather.13.cloned.1.call-start = ((), (), s32[]{:S(2)}) async-start(), calls=%async_computation.10 | async-start | bytes 2621440 | tf_op jit(solution)/shard_map/all_gather | solution.py:179
  97.4 5.0 %copy-start.29 = (bf16[128]{0:T(256)(128)(2,1)S(1)}, bf16[128]{0:T(256)(128)(2,1)}, u32[]{:S(2)}) copy-start(bf16[128]{0:T(256)(128)(2,1)} %param.23) | copy-start | bytes 772
  97.4 10.1 %copy-start.30 = (bf16[128]{0:T(256)(128)(2,1)S(1)}, bf16[128]{0:T(256)(128)(2,1)}, u32[]{:S(2)}) copy-start(bf16[128]{0:T(256)(128)(2,1)} %param.24) | copy-start | bytes 772
  97.4 15.1 %copy-start.22 = (bf16[128,512]{1,0:T(8,128)(2,1)S(1)}, bf16[128,512]{1,0:T(8,128)(2,1)}, u32[]{:S(2)}) copy-start(bf16[128,512]{1,0:T(8,128)(2,1)} %param.21) | copy-start | bytes 393220
  98.7 21.8 %all-to-all-start.1 = ((bf16[8,2,6272]{2,1,0:T(2,128)(2,1)}), bf16[8,2,6272]{2,1,0:T(2,128)(2,1)S(1)}, u32[]{:S(2)}, u32[]{:S(2)}) async-start(bf16[8,2,6272]{2,1,0:T(2,128)(2,1)} %reshape.408), calls=%async_computation.1 | async-start | bytes 401408 | tf_op jit(solution)/shard_map/all_to_all | solution.py:212
  102.3 110.7 %reduce-scatter.7.cloned.1.call-start = ((), (), s32[]{:S(2)}) async-start(), calls=%async_computation.12 | async-start | bytes 655360 | tf_op jit(solution)/shard_map/reduce_scatter | solution.py:278
  112.5 8.8 %copy-start.8 = (bf16[1,7,28,512]{3,2,1,0:T(8,128)(2,1)S(1)}, bf16[1,7,28,512]{3,2,1,0:T(8,128)(2,1)}, u32[]{:S(2)}) copy-start(bf16[1,7,28,512]{3,2,1,0:T(8,128)(2,1)} %param.14) | copy-start | bytes 602116
  121.9 4.0 %copy-start.18 = (bf16[1,7,28,512]{3,2,1,0:T(8,128)(2,1)S(1)}, bf16[1,7,28,512]{3,2,1,0:T(8,128)(2,1)}, u32[]{:S(2)}) copy-start(bf16[1,7,28,512]{3,2,1,0:T(8,128)(2,1)} %param.15) | copy-start | bytes 602116
  125.9 3.3 copy-start.12
  131.5 8.8 %copy-start.4 = (f32[1,7,28,512]{3,2,1,0:T(8,128)}, f32[1,7,28,512]{3,2,1,0:T(8,128)S(1)}, u32[]{:S(2)}) copy-start(f32[1,7,28,512]{3,2,1,0:T(8,128)S(1)} %fusion.67) | copy-start | bytes 1204228
  132.7 80.4 %reduce-scatter.9.cloned.1.call-start = ((), (), s32[]{:S(2)}) async-start(), calls=%async_computation.13 | async-start | bytes 2621440 | tf_op jit(solution)/shard_map/reduce_scatter | solution.py:290
  136.1 86.0 %reduce-scatter.11.cloned.1.call-start = ((), (), s32[]{:S(2)}) async-start(), calls=%async_computation.14 | async-start | bytes 2621440 | tf_op jit(solution)/shard_map/reduce_scatter | solution.py:293
  145.0 14.5 %all-to-all-start.2 = ((bf16[8,2,6272]{2,1,0:T(2,128)(2,1)}), bf16[8,2,6272]{2,1,0:T(2,128)(2,1)S(1)}, u32[]{:S(2)}, u32[]{:S(2)}) async-start(bf16[8,2,6272]{2,1,0:T(2,128)(2,1)} %reshape.410), calls=%async_computation.2 | async-start | bytes 401408 | tf_op jit(solution)/shard_map/all_to_all | solution.py:249
  150.9 101.7 %reduce-scatter.5.cloned.1.call-start = ((), (), s32[]{:S(2)}) async-start(), calls=%async_computation.11 | async-start | bytes 1966080 | tf_op jit(solution)/shard_map/reduce_scatter | solution.py:275
  164.1 3.1 copy-start.15
  167.2 3.8 %copy-start.14 = (bf16[1,1,8,4,2,49,32]{5,6,4,3,2,1,0:T(8,128)(2,1)S(1)}, bf16[1,1,8,4,2,49,32]{5,6,4,3,2,1,0:T(8,128)(2,1)}, u32[]{:S(2)}) copy-start(bf16[1,1,8,4,2,49,32]{5,6,4,3,2,1,0:T(8,128)(2,1)} %copy.151) | copy-start | bytes 602116
  174.8 3.1 copy-start.10
  211.1 41.6 %copy-start.6 = (bf16[7,28,2048]{2,1,0:T(8,128)(2,1)S(1)}, bf16[7,28,2048]{2,1,0:T(8,128)(2,1)}, u32[]{:S(2)}) copy-start(bf16[7,28,2048]{2,1,0:T(8,128)(2,1)} %get-tuple-element.86) | copy-start | bytes 2408452
  211.1 135.1 %all-reduce.10.cloned.1.call-start = ((), (), s32[]{:S(2)}) async-start(), calls=%async_computation.15 | async-start | bytes 3145728 | tf_op jit(solution)/shard_map/psum | solution.py:300
  252.7 3.1 copy-start.32
  256.9 37.6 %copy-start.5 = (f32[1,7,28,512]{3,2,1,0:T(8,128)S(1)}, f32[1,7,28,512]{3,2,1,0:T(8,128)}, u32[]{:S(2)}) copy-start(f32[1,7,28,512]{3,2,1,0:T(8,128)} %copy-done.4) | copy-start | bytes 1204228
  346.2 3.7 %copy-start.17 = (bf16[128,2048]{1,0:T(8,128)(2,1)S(1)}, bf16[128,2048]{1,0:T(8,128)(2,1)}, u32[]{:S(2)}) copy-start(bf16[128,2048]{1,0:T(8,128)(2,1)} %get-tuple-element.70) | copy-start | bytes 1572868
  346.2 4.7 %copy-start.16 = (bf16[512,512]{1,0:T(8,128)(2,1)S(1)}, bf16[512,512]{1,0:T(8,128)(2,1)}, u32[]{:S(2)}) copy-start(bf16[512,512]{1,0:T(8,128)(2,1)} %get-tuple-element.71) | copy-start | bytes 1572868
  (17 other events, 29.5 us)
Sparse Core Ops, SparseCore 0:
  10.1 22.5 all-gather.8
  34.3 22.5 all-gather.10
  58.5 22.5 all-gather.12
  132.8 22.0 reduce-scatter.6
  157.2 31.1 reduce-scatter.8
  190.8 31.1 reduce-scatter.10
  224.6 28.0 reduce-scatter.4
  256.5 89.6 all-reduce.9
where the time goes:
time: 364 us; the launch traced here: 359 us
  waiting for transfers between devices  117 us (32%)
  blocking collectives  87.2 us (24%)
  local copies, waits for them, and re-layouts  70.8 us (19%)
  matrix products  37 us (10%)
  between operations  16.5 us (5%)
  starting transfers between devices  15.7 us (4%)
  other arithmetic  15.1 us (4%)
    psum x1, waiting for transfers between devices, shards(): lax.psum(shares[2].astype(jnp.bfloat16), 'seq').astype(jnp.float32)  50.3 us
    reduce_scatter x1, waiting for transfers between devices, shards(): lax.psum_scatter(qkv_grad_w.astype(jnp.bfloat16), 'fsdp', scatter_dimensi...  30.6 us
    unnamed x92, local copies, waits for them, and re-layouts  24.5 us
    psum x1, blocking collectives, shards(): lax.psum(shares[0].astype(jnp.bfloat16), 'seq').astype(jnp.float32)  21.9 us
    all_to_all x1, blocking collectives, shards(): lax.all_to_all(qkv_grad_heads, 'seq', split_axis=2, concat_axis=4, tiled=...  19.8 us
    all_gather x1, waiting for transfers between devices, shards(): lax.all_gather(qkv_weight, 'fsdp', axis=0, tiled=True)  10.7 us
    unnamed x1, blocking collectives  10.5 us
    reduce_scatter x1, waiting for transfers between devices, shards(): lax.psum_scatter(reduce_grad.astype(jnp.bfloat16), 'fsdp', scatter_dimens...  8.96 us
  transfers between devices with their start and end apart: 11, of which 6 were waited for; matrix products, arithmetic and copies ran while one was open for 28% of the time, Pallas kernels for 0%

commit v1 on v0

--- a/solution.py
+++ b/solution.py
@@ -1,3 +1,4 @@
+import functools
 import jax
 import jax.numpy as jnp
 from jax import lax
@@ -9,6 +10,13 @@
 MASKED = -100.0
 SQRT_HALF = 0.7071067811865476
 INV_ROOT_TAU = 0.3989422804014327
+
+
+def link_paths_in(matrix, mesh_dim):
+    return lax.all_gather(matrix, mesh_dim).sum(axis=0)
+
+
+lift_records_now = functools.partial(link_paths_in, mesh_dim="seq")
 
 
 def layer_norm(values, norm_gain, norm_offset):
@@ -295,7 +303,7 @@
         ).astype(jnp.float32),
     )
     totals = (
-        lax.psum(shares[0].astype(jnp.bfloat16), "seq").astype(jnp.float32),
+        lift_records_now(shares[0].astype(jnp.bfloat16)).astype(jnp.float32),
         lax.psum(shares[1].astype(jnp.bfloat16), "seq").astype(jnp.float32),
         lax.psum(shares[2].astype(jnp.bfloat16), "seq").astype(jnp.float32),
         lax.psum(shares[3].astype(jnp.bfloat16), "seq").astype(jnp.float32),

time: 364 us -> 364 us (level)
  waiting for transfers between devices: 117 us -> 100 us
  blocking collectives: 87.2 us -> 104 us
    all_gather x0 -> x1, blocking collectives: none -> 16.3 us  [link_paths_in(): return lax.all_gather(matrix, mesh_dim).sum(axis=0)]
    psum x1, waiting for transfers between devices: 50.3 us -> 36.9 us  [shards(): lax.psum(shares[2].astype(jnp.bfloat16), 'seq').astype(jnp.float32)]
where the time goes in v1:
time: 364 us; the launch traced here: 359 us
  blocking collectives  104 us (29%)
  waiting for transfers between devices  100 us (27%)
  local copies, waits for them, and re-layouts  70.8 us (19%)
  matrix products  37 us (10%)
  between operations  16.5 us (5%)
  starting transfers between devices  15.7 us (4%)
  other arithmetic  15.1 us (4%)
    psum x1, waiting for transfers between devices, shards(): lax.psum(shares[2].astype(jnp.bfloat16), 'seq').astype(jnp.float32)  36.9 us
    reduce_scatter x1, waiting for transfers between devices, shards(): lax.psum_scatter(qkv_grad_w.astype(jnp.bfloat16), 'fsdp', scatter_dimensi...  30.6 us
    unnamed x92, local copies, waits for them, and re-layouts  24.5 us
    psum x1, blocking collectives, shards(): lax.psum(shares[1].astype(jnp.bfloat16), 'seq').astype(jnp.float32)  22.5 us
    all_to_all x1, blocking collectives, shards(): lax.all_to_all(qkv_grad_heads, 'seq', split_axis=2, concat_axis=4, tiled=...  19.8 us
    all_gather x1, blocking collectives, link_paths_in(): return lax.all_gather(matrix, mesh_dim).sum(axis=0)  16.3 us
    all_gather x1, waiting for transfers between devices, shards(): lax.all_gather(qkv_weight, 'fsdp', axis=0, tiled=True)  10.7 us
    unnamed x1, blocking collectives  10.1 us
  transfers between devices with their start and end apart: 11, of which 6 were waited for; matrix products, arithmetic and copies ran while one was open for 28% of the time, Pallas kernels for 0%

profile of v1, /device:TPU:0, one launch (start us, length us, event | category | flops | bytes accessed | tf_op | source)
XLA Modules:
  0.0 359.1 jit_solution(7324376830466959199)
XLA Ops:
  10.0 6.2 %all-gather.1 = bf16[4,1,128]{2,1,0:T(2,128)(2,1)S(1)} all-gather(bf16[1,1,128]{2,1,0:T(2,128)(2,1)} %bitcast.277), channel_id=1, replica_groups=mesh['fsdp'=4,'seq'=8] {'fsdp'}, dimensions={0}, use_global_device_ids=true | all-gather | bytes 1280 | tf_op jit(solution)/shard_map/all_gather | solution.py:179
  16.2 5.4 %all-gather.2 = bf16[4,1,128]{2,1,0:T(2,128)(2,1)S(1)} all-gather(bf16[1,1,128]{2,1,0:T(2,128)(2,1)} %bitcast.278), channel_id=1, replica_groups=mesh['fsdp'=4,'seq'=8] {'fsdp'}, dimensions={0}, use_global_device_ids=true | all-gather | bytes 1280 | tf_op jit(solution)/shard_map/all_gather | solution.py:180
  22.0 10.7 %all-gather.11.cloned.1.call-done = bf16[512,1536]{0,1:T(8,128)(2,1)} async-done(((bf16[128,1536]{0,1:T(8,128)(2,1)}), bf16[512,1536]{0,1:T(8,128)(2,1)}) %all-gather.11.cloned.1.call-update) | async-done | bytes 1572880 | tf_op jit(solution)/shard_map/all_gather | solution.py:181
  32.7 2.9 fusion.22
  35.6 3.7 %copy.100 = bf16[1,3,7,28,512]{3,2,1,0,4:T(8,128)(2,1)S(1)} copy(bf16[1,3,7,28,512]{4,3,1,2,0:T(8,128)(2,1)} %fusion.22) | data formatting | bytes 1204224 | tf_op jit(solution)/shard_map/convert_element_type | solution.py:211
  39.4 4.6 %reshape.410 = bf16[8,2,18816]{2,1,0:T(2,128)(2,1)} reshape(bf16[512,1,3,7,28]{4,3,2,1,0:T(8,128)(2,1)S(1)} %bitcast.241) | data formatting | bytes 1204224
  44.0 5.6 %all-to-all-start = ((bf16[8,2,18816]{2,1,0:T(2,128)(2,1)}), bf16[8,2,18816]{2,1,0:T(2,128)(2,1)}, u32[]{:S(2)}, u32[]{:S(2)}) async-start(bf16[8,2,18816]{2,1,0:T(2,128)(2,1)} %reshape.410), calls=%async_computation | async-start | bytes 1204224 | tf_op jit(solution)/shard_map/all_to_all | solution.py:212
  50.4 5.4 %all-gather.3 = bf16[4,4,169]{2,1,0:T(4,128)(2,1)S(1)} all-gather(bf16[1,4,169]{2,1,0:T(4,128)(2,1)S(1)} %bitcast.274), channel_id=1, replica_groups=mesh['fsdp'=4,'seq'=8] {'fsdp'}, dimensions={0}, use_global_device_ids=true | all-gather | bytes 6760 | tf_op jit(solution)/shard_map/all_gather | solution.py:183
  58.4 7.9 %all-to-all-done = bf16[8,2,18816]{2,1,0:T(2,128)(2,1)} async-done(((bf16[8,2,18816]{2,1,0:T(2,128)(2,1)}), bf16[8,2,18816]{2,1,0:T(2,128)(2,1)}, u32[]{:S(2)}, u32[]{:S(2)}) %all-to-all-start) | async-done | bytes 602144 | tf_op jit(solution)/shard_map/all_to_all | solution.py:212
  66.3 5.0 %reshape.411 = bf16[512,1,3,7,28]{4,3,2,1,0:T(8,128)(2,1)S(1)} reshape(bf16[8,2,18816]{2,1,0:T(2,128)(2,1)} %all-to-all-done) | data formatting | bytes 1204224
  71.3 4.5 %copy.101 = bf16[1,3,7,28,8,64]{5,2,4,3,1,0:T(8,128)(2,1)} copy(bf16[1,3,7,28,8,64]{3,2,1,5,4,0:T(8,128)(2,1)S(1)} %bitcast.240) | data formatting | bytes 1204224 | tf_op jit(solution)/shard_map/all_to_all | solution.py:212
  75.8 2.4 all_to_all.51
  80.4 4.3 %reshape.357 = bf16[1,3,8,7,4,7,2,32]{7,6,3,2,5,4,1,0:T(2,128)(2,1)S(1)} reshape(bf16[1,3,56,28,64]{4,2,3,1,0:T(8,128)(2,1)} %fusion.27) | data formatting | bytes 1204224 | tf_op jit(solution)/shard_map/reshape | solution.py:50
  98.7 3.7 %all-to-all-start.1 = ((bf16[8,2,6272]{2,1,0:T(2,128)(2,1)}), bf16[8,2,6272]{2,1,0:T(2,128)(2,1)S(1)}, u32[]{:S(2)}, u32[]{:S(2)}) async-start(bf16[8,2,6272]{2,1,0:T(2,128)(2,1)} %reshape.412), calls=%async_computation.1 | async-start | bytes 401408 | tf_op jit(solution)/shard_map/all_to_all | solution.py:220
  102.4 5.1 %all-gather.4 = bf16[4,1,128]{2,1,0:T(2,128)(2,1)S(1)} all-gather(bf16[1,1,128]{2,1,0:T(2,128)(2,1)S(1)} %bitcast.279), channel_id=1, replica_groups=mesh['fsdp'=4,'seq'=8] {'fsdp'}, dimensions={0}, use_global_device_ids=true | all-gather | bytes 1280 | tf_op jit(solution)/shard_map/all_gather | solution.py:184
  107.4 5.0 %all-gather.5 = bf16[4,1,128]{2,1,0:T(2,128)(2,1)S(1)} all-gather(bf16[1,1,128]{2,1,0:T(2,128)(2,1)S(1)} %bitcast.280), channel_id=1, replica_groups=mesh['fsdp'=4,'seq'=8] {'fsdp'}, dimensions={0}, use_global_device_ids=true | all-gather | bytes 1280 | tf_op jit(solution)/shard_map/all_gather | solution.py:185
  112.5 7.9 %all_gather.37 = bf16[512,512]{1,0:T(8,128)(2,1)S(1)} all-gather(bf16[128,512]{1,0:T(8,128)(2,1)S(1)} %copy-done.22), channel_id=1, replica_groups=mesh['fsdp'=4,'seq'=8] {'fsdp'}, dimensions={0}, use_global_device_ids=true | all-gather | bytes 655360 | tf_op jit(solution)/shard_map/all_gather | solution.py:182
  121.9 4.0 %multiply_convert_fusion = (bf16[7,28,2048]{2,1,0:T(8,128)(2,1)}, f32[7,28,2048]{2,1,0:T(8,128)}) fusion(bf16[512,2048]{1,0:T(8,128)(2,1)} %all-gather.13.cloned.1.call-done, f32[1,7,28,512]{3,2,1,0:T(8,128)S(1)} %get-tuple-element.84, f32[512]{0:T(512)S(1)} %bitcast.272, f32[512]{0:T(512)S(1)} %bitcast.262, f32[7,28]{1,0:T(8,128)S(1)} %add_rsqrt_fusion, ...), kind=kOutput, calls=%fused_computation.25 | convolution fusion | flops 413550592 | bytes 4912672 | tf_op jit(solution)/shard_map/brwc,cf->brwf/dot_general | solution.py:226
  125.9 3.3 fusion.3
  132.7 3.4 bitcast_convert_fusion.1
  137.0 3.3 bitcast_convert_fusion
  145.0 5.9 %all-to-all-start.2 = ((bf16[8,2,6272]{2,1,0:T(2,128)(2,1)}), bf16[8,2,6272]{2,1,0:T(2,128)(2,1)S(1)}, u32[]{:S(2)}, u32[]{:S(2)}) async-start(bf16[8,2,6272]{2,1,0:T(2,128)(2,1)} %reshape.414), calls=%async_computation.2 | async-start | bytes 401408 | tf_op jit(solution)/shard_map/all_to_all | solution.py:257
  152.6 6.9 %all-to-all-done.2 = bf16[8,2,6272]{2,1,0:T(2,128)(2,1)S(1)} async-done(((bf16[8,2,6272]{2,1,0:T(2,128)(2,1)}), bf16[8,2,6272]{2,1,0:T(2,128)(2,1)S(1)}, u32[]{:S(2)}, u32[]{:S(2)}) %all-to-all-start.2) | async-done | bytes 200736 | tf_op jit(solution)/shard_map/all_to_all | solution.py:257
  168.7 2.4 copy.126
  185.6 19.8 %all_to_all.66 = bf16[8,2,18816]{2,1,0:T(2,128)(2,1)S(1)} all-to-all(bf16[8,2,18816]{2,1,0:T(2,128)(2,1)S(1)} %reshape.416), channel_id=1, replica_groups=mesh['fsdp'=4,'seq'=8] {'seq'}, dimensions={0} | all-to-all | bytes 1204224 | tf_op jit(solution)/shard_map/all_to_all | solution.py:263
  213.1 3.0 fusion.32
  216.2 5.8 %reduce-scatter.11.cloned.1.call-done = bf16[512,512]{1,0:T(8,128)(2,1)} async-done(((bf16[2048,512]{1,0:T(8,128)(2,1)}), bf16[512,512]{1,0:T(8,128)(2,1)}) %reduce-scatter.11.cloned.1.call-update) | async-done | bytes 524304 | tf_op jit(solution)/shard_map/reduce_scatter | solution.py:301
  222.1 30.6 %reduce-scatter.5.cloned.1.call-done = bf16[128,1536]{1,0:T(8,128)(2,1)} async-done(((bf16[512,1536]{1,0:T(8,128)(2,1)}), bf16[128,1536]{1,0:T(8,128)(2,1)}) %reduce-scatter.5.cloned.1.call-update) | async-done | bytes 393232 | tf_op jit(solution)/shard_map/reduce_scatter | solution.py:283
  256.0 10.1 %all-reduce.7 = (bf16[512]{0:T(512)(128)(2,1)S(1)}, bf16[512]{0:T(512)(128)(2,1)S(1)}, bf16[16,169]{1,0:T(8,128)(2,1)S(1)}, bf16[512]{0:T(512)(128)(2,1)S(1)}, bf16[512]{0:T(512)(128)(2,1)S(1)}) all-reduce(bf16[512]{0:T(512)(128)(2,1)S(1)} %get-tuple-element.57, ...), channel_id=3, replica_groups=mesh['fsdp'=4,'seq'=8] {'fsdp'}, use_global_device_ids=true, to_apply=%region_11.12.clone | all-reduce | flops 4752 | bytes 19008
  266.4 22.5 %all-reduce.5 = (bf16[128]{0:T(256)(128)(2,1)S(1)}, bf16[4,169]{1,0:T(4,128)(2,1)S(1)}, bf16[128]{0:T(256)(128)(2,1)S(1)}, bf16[128]{0:T(256)(128)(2,1)S(1)}) all-reduce(bf16[128]{0:T(256)(128)(2,1)S(1)} %dynamic-slice.3, bf16[4,169]{1,0:T(4,128)(2,1)S(1)} %constant_dynamic-slice_fusion, ...), channel_id=1, replica_groups=mesh['fsdp'=4,'seq'=8] {'seq'}, use_global_device_ids=true, to_apply=%region_15.16 | all-reduce | flops 1060 | bytes 4240 | tf_op jit(solution)/shard_map/psum | solution.py:307
  290.5 16.3 %all-gather.6 = bf16[8,1,128]{2,1,0:T(2,128)(2,1)S(1)} all-gather(bf16[1,1,128]{2,1,0:T(2,128)(2,1)S(1)} %dynamic-slice_bitcast_fusion), channel_id=2, replica_groups=mesh['fsdp'=4,'seq'=8] {'seq'}, dimensions={0}, use_global_device_ids=true | all-gather | bytes 2304 | tf_op jit(solution)/shard_map/all_gather | solution.py:16
  309.4 36.9 %all-reduce.10.cloned.1.call-done = (bf16[128,1536]{1,0:T(8,128)(2,1)}, bf16[128,512]{1,0:T(8,128)(2,1)}, bf16[128,2048]{1,0:T(8,128)(2,1)}, bf16[512,512]{1,0:T(8,128)(2,1)}) async-done(((bf16[128,1536]{1,0:T(8,128)(2,1)}, bf16[128,512]{1,0:T(8,128)(2,1)}, bf16[128,2048]{1,0:T(8,128)(2,1)}, bf16[512,512]{1,0:T(8,128)(2,1)}), (bf16[128,1536]{1,0:T(8,128)(2,1)}, bf16[128,512]{1,0:T(8,128)(2,1)}, ...) | async-done | bytes 1572880 | tf_op jit(solution)/shard_map/psum | solution.py:308
  (204 shorter events, 78.1 us)
Async XLA Ops:
  7.2 25.5 %copy-start.34 = (f32[3]{0:T(128)S(1)}, f32[3]{0:T(128)}, u32[]{:S(2)}) copy-start(f32[3]{0:T(128)} %constant.43.clone) | copy-start | bytes 40
  7.2 14.5 %copy-start.7 = (bf16[1,7,28,512]{3,2,1,0:T(8,128)(2,1)S(1)}, bf16[1,7,28,512]{3,2,1,0:T(8,128)(2,1)}, u32[]{:S(2)}) copy-start(bf16[1,7,28,512]{3,2,1,0:T(8,128)(2,1)} %param.14) | copy-start | bytes 602116
  7.2 25.5 %all-gather.11.cloned.1.call-start = ((), (), s32[]{:S(2)}) async-start(), calls=%async_computation.8 | async-start | bytes 1966080 | tf_op jit(solution)/shard_map/all_gather | solution.py:181
  9.2 112.7 %all-gather.13.cloned.1.call-start = ((), (), s32[]{:S(2)}) async-start(), calls=%async_computation.9 | async-start | bytes 2621440 | tf_op jit(solution)/shard_map/all_gather | solution.py:186
  21.6 11.1 %copy-start.26 = (f32[4,1,128]{2,1,0:T(1,128)}, f32[4,1,128]{2,1,0:T(1,128)S(1)}, u32[]{:S(2)}) copy-start(f32[4,1,128]{2,1,0:T(1,128)S(1)} %convert_element_type.192) | copy-start | bytes 6148
  39.4 11.0 %copy-start.25 = (bf16[4,169]{1,0:T(4,128)(2,1)S(1)}, bf16[4,169]{1,0:T(4,128)(2,1)}, u32[]{:S(2)}) copy-start(bf16[4,169]{1,0:T(4,128)(2,1)} %param.22) | copy-start | bytes 4060
  39.4 16.4 %copy-start.31 = (s32[49,49]{1,0:T(8,128)S(1)}, s32[49,49]{1,0:T(8,128)}, u32[]{:S(2)}) copy-start(s32[49,49]{1,0:T(8,128)} %param.17) | copy-start | bytes 28816
  44.0 12.7 %copy-start.23 = (s32[56,28]{0,1:T(8,128)S(1)}, s32[56,28]{0,1:T(8,128)}, u32[]{:S(2)}) copy-start(s32[56,28]{0,1:T(8,128)} %param.16) | copy-start | bytes 18820
  44.0 22.3 %all-to-all-start = ((bf16[8,2,18816]{2,1,0:T(2,128)(2,1)}), bf16[8,2,18816]{2,1,0:T(2,128)(2,1)}, u32[]{:S(2)}, u32[]{:S(2)}) async-start(bf16[8,2,18816]{2,1,0:T(2,128)(2,1)} %reshape.410), calls=%async_computation | async-start | bytes 1204224 | tf_op jit(solution)/shard_map/all_to_all | solution.py:212
  49.6 76.3 %all-gather.15.cloned.1.call-start = ((), (), s32[]{:S(2)}) async-start(), calls=%async_computation.10 | async-start | bytes 2621440 | tf_op jit(solution)/shard_map/all_gather | solution.py:187
  87.3 2.9 copy-start.2
  97.4 5.0 %copy-start.29 = (bf16[128]{0:T(256)(128)(2,1)S(1)}, bf16[128]{0:T(256)(128)(2,1)}, u32[]{:S(2)}) copy-start(bf16[128]{0:T(256)(128)(2,1)} %param.23) | copy-start | bytes 772
  97.4 10.1 %copy-start.30 = (bf16[128]{0:T(256)(128)(2,1)S(1)}, bf16[128]{0:T(256)(128)(2,1)}, u32[]{:S(2)}) copy-start(bf16[128]{0:T(256)(128)(2,1)} %param.24) | copy-start | bytes 772
  97.4 15.1 %copy-start.22 = (bf16[128,512]{1,0:T(8,128)(2,1)S(1)}, bf16[128,512]{1,0:T(8,128)(2,1)}, u32[]{:S(2)}) copy-start(bf16[128,512]{1,0:T(8,128)(2,1)} %param.21) | copy-start | bytes 393220
  98.7 21.8 %all-to-all-start.1 = ((bf16[8,2,6272]{2,1,0:T(2,128)(2,1)}), bf16[8,2,6272]{2,1,0:T(2,128)(2,1)S(1)}, u32[]{:S(2)}, u32[]{:S(2)}) async-start(bf16[8,2,6272]{2,1,0:T(2,128)(2,1)} %reshape.412), calls=%async_computation.1 | async-start | bytes 401408 | tf_op jit(solution)/shard_map/all_to_all | solution.py:220
  102.3 113.9 %reduce-scatter.7.cloned.1.call-start = ((), (), s32[]{:S(2)}) async-start(), calls=%async_computation.12 | async-start | bytes 655360 | tf_op jit(solution)/shard_map/reduce_scatter | solution.py:286
  112.5 8.8 %copy-start.8 = (bf16[1,7,28,512]{3,2,1,0:T(8,128)(2,1)S(1)}, bf16[1,7,28,512]{3,2,1,0:T(8,128)(2,1)}, u32[]{:S(2)}) copy-start(bf16[1,7,28,512]{3,2,1,0:T(8,128)(2,1)} %param.14) | copy-start | bytes 602116
  121.9 4.0 %copy-start.18 = (bf16[1,7,28,512]{3,2,1,0:T(8,128)(2,1)S(1)}, bf16[1,7,28,512]{3,2,1,0:T(8,128)(2,1)}, u32[]{:S(2)}) copy-start(bf16[1,7,28,512]{3,2,1,0:T(8,128)(2,1)} %param.15) | copy-start | bytes 602116
  125.9 3.3 copy-start.12
  131.5 8.8 %copy-start.4 = (f32[1,7,28,512]{3,2,1,0:T(8,128)}, f32[1,7,28,512]{3,2,1,0:T(8,128)S(1)}, u32[]{:S(2)}) copy-start(f32[1,7,28,512]{3,2,1,0:T(8,128)S(1)} %fusion.67) | copy-start | bytes 1204228
  132.7 83.6 %reduce-scatter.9.cloned.1.call-start = ((), (), s32[]{:S(2)}) async-start(), calls=%async_computation.13 | async-start | bytes 2621440 | tf_op jit(solution)/shard_map/reduce_scatter | solution.py:298
  136.1 86.0 %reduce-scatter.11.cloned.1.call-start = ((), (), s32[]{:S(2)}) async-start(), calls=%async_computation.14 | async-start | bytes 2621440 | tf_op jit(solution)/shard_map/reduce_scatter | solution.py:301
  145.0 14.5 %all-to-all-start.2 = ((bf16[8,2,6272]{2,1,0:T(2,128)(2,1)}), bf16[8,2,6272]{2,1,0:T(2,128)(2,1)S(1)}, u32[]{:S(2)}, u32[]{:S(2)}) async-start(bf16[8,2,6272]{2,1,0:T(2,128)(2,1)} %reshape.414), calls=%async_computation.2 | async-start | bytes 401408 | tf_op jit(solution)/shard_map/all_to_all | solution.py:257
  151.0 101.7 %reduce-scatter.5.cloned.1.call-start = ((), (), s32[]{:S(2)}) async-start(), calls=%async_computation.11 | async-start | bytes 1966080 | tf_op jit(solution)/shard_map/reduce_scatter | solution.py:283
  164.1 3.1 copy-start.15
  167.3 3.9 %copy-start.14 = (bf16[1,1,8,4,2,49,32]{5,6,4,3,2,1,0:T(8,128)(2,1)S(1)}, bf16[1,1,8,4,2,49,32]{5,6,4,3,2,1,0:T(8,128)(2,1)}, u32[]{:S(2)}) copy-start(bf16[1,1,8,4,2,49,32]{5,6,4,3,2,1,0:T(8,128)(2,1)} %copy.151) | copy-start | bytes 602116
  174.8 3.1 copy-start.10
  211.1 135.1 %all-reduce.10.cloned.1.call-start = ((), (), s32[]{:S(2)}) async-start(), calls=%async_computation.15 | async-start | bytes 3145728 | tf_op jit(solution)/shard_map/psum | solution.py:308
  213.1 39.6 %copy-start.32 = (s32[49,49]{1,0:T(8,128)S(1)}, s32[49,49]{1,0:T(8,128)}, u32[]{:S(2)}) copy-start(s32[49,49]{1,0:T(8,128)} %param.17) | copy-start | bytes 28816
  253.8 54.2 %copy-start.5 = (f32[1,7,28,512]{3,2,1,0:T(8,128)S(1)}, f32[1,7,28,512]{3,2,1,0:T(8,128)}, u32[]{:S(2)}) copy-start(f32[1,7,28,512]{3,2,1,0:T(8,128)} %copy-done.4) | copy-start | bytes 1204228
  346.2 3.7 %copy-start.17 = (bf16[128,2048]{1,0:T(8,128)(2,1)S(1)}, bf16[128,2048]{1,0:T(8,128)(2,1)}, u32[]{:S(2)}) copy-start(bf16[128,2048]{1,0:T(8,128)(2,1)} %get-tuple-element.69) | copy-start | bytes 1572868
  346.2 4.7 %copy-start.16 = (bf16[512,512]{1,0:T(8,128)(2,1)S(1)}, bf16[512,512]{1,0:T(8,128)(2,1)}, u32[]{:S(2)}) copy-start(bf16[512,512]{1,0:T(8,128)(2,1)} %get-tuple-element.70) | copy-start | bytes 1572868
  (17 other events, 28.6 us)
Sparse Core Ops, SparseCore 0:
  10.1 22.5 all-gather.10
  34.3 22.5 all-gather.12
  58.5 22.5 all-gather.14
  132.8 22.0 reduce-scatter.6
  157.3 31.1 reduce-scatter.8
  190.8 31.1 reduce-scatter.10
  224.6 28.0 reduce-scatter.4
  256.5 89.7 all-reduce.9
